TPU v7x, 32 devices: a whole 2x2x4 slice. The times are simulated.
32 devices in a mesh: seq: 8 (over z, x), qblk: 4 (over y, core).
Axes of the slice: x: 2, y: 2, z: 4, core: 2. Of those that a mesh axis runs over, the one named last changes fastest.
Arguments:
- queries: bfloat16 [4096, 8192], P(('seq', 'qblk')), may hold values from -33 to 33
- key_states: bfloat16 [4096, 1024], P(('seq', 'qblk')), may hold values from -6 to 6
- value_states: bfloat16 [4096, 1024], P(('seq', 'qblk')), may hold values from -6 to 6
- block_list: int32 [64, 32, 16], replicated, may hold values from 0 to 31, as said below
- block_count: int32 [64, 32], replicated, may hold values from 1 to 16, as said below
Outputs:
- attended: bfloat16 [4096, 8192], P(('seq', 'qblk'))
Inputs may be any that keep to these rules, and one draw needn't show every extreme that they name: `block_list`: for each head and query block, the first block_count entries are distinct key blocks no later than the query block, among them the query block itself; the remaining entries are 0. block_count[h, i] <= i + 1.
All inputs are finite; a program needn't handle non-finite values.
Results may differ from a plain program's by a relative error of at most 0.0044.
Values may be sent and summed in bfloat16 or wider, within the bound.
A program may use at most 64 MiB of HBM per device.

v0:
```python
import jax
import jax.numpy as jnp
import numpy as np
from jax import lax
from jax.sharding import PartitionSpec as P

H = 64
KVH = 8
HEAD_SIZE = 128
BLK = 128
MAXB = 16


def shards(queries, key_states, value_states, block_list, block_count):
    n_seq = lax.axis_size("seq")
    n_qblk = lax.axis_size("qblk")
    local_rows = queries.shape[0]
    per_dev = local_rows // BLK
    per_seq = H // n_seq
    group_size = H // KVH
    seq_id = lax.axis_index("seq")
    qblk_id = lax.axis_index("qblk")
    score_scale = HEAD_SIZE ** (-0.5)
    by_slot = queries.reshape(local_rows, n_seq, per_seq * HEAD_SIZE)
    q_mine = lax.all_to_all(by_slot, "seq", split_axis=1, concat_axis=0, tiled=True)
    kv_pairs = jnp.concatenate(
        [
            key_states.reshape(local_rows, KVH, HEAD_SIZE),
            value_states.reshape(local_rows, KVH, HEAD_SIZE),
        ],
        axis=2,
    )
    dest_group = np.arange(n_seq) * per_seq // group_size
    kv_chosen = kv_pairs[:, dest_group, :]
    spread = jnp.broadcast_to(
        kv_chosen[:, :, None, :], (local_rows, n_seq, n_qblk, 2 * HEAD_SIZE)
    ).reshape(local_rows, n_seq * n_qblk, 2 * HEAD_SIZE)
    arrived = lax.all_to_all(spread, ("seq", "qblk"), split_axis=1, concat_axis=0, tiled=True)
    kv_blocks = arrived.reshape(-1, BLK, 2 * HEAD_SIZE)
    block_lists = lax.dynamic_slice_in_dim(block_list, seq_id * per_seq, per_seq, 0)
    block_counts = lax.dynamic_slice_in_dim(block_count, seq_id * per_seq, per_seq, 0)
    q_blocks = q_mine.reshape(n_seq * per_dev, BLK, per_seq, HEAD_SIZE)
    local_ids = jnp.arange(n_seq * per_dev, dtype=jnp.int32)
    query_ids = (local_ids // per_dev * n_qblk + qblk_id) * per_dev + local_ids % per_dev
    inner_pos = jnp.arange(BLK, dtype=jnp.int32)
    slot_ids = jnp.arange(MAXB, dtype=jnp.int32)[None, None, :, None]

    def attend(block_item):
        q_tile, query_block = block_item
        indices = block_lists[:, query_block, :]
        counts_now = block_counts[:, query_block]
        key_value_tiles = kv_blocks[indices]
        attention_scores = (
            jnp.einsum(
                "qhd,hmkd->hqmk",
                q_tile,
                key_value_tiles[..., :HEAD_SIZE],
                preferred_element_type=jnp.float32,
            )
            * score_scale
        )
        key_pos = indices[:, None, :, None] * BLK + inner_pos[None, None, None, :]
        query_pos = query_block * BLK + inner_pos[None, :, None, None]
        usable = (slot_ids < counts_now[:, None, None, None]) & (key_pos <= query_pos)
        attention_scores = jnp.where(usable, attention_scores, -jnp.inf)
        highest = jnp.max(attention_scores, axis=(2, 3), keepdims=True)
        weights = jnp.exp(attention_scores - highest)
        weight_sum = jnp.sum(weights, axis=(2, 3))
        combined_output = jnp.einsum(
            "hqmk,hmkd->qhd",
            weights.astype(jnp.bfloat16),
            key_value_tiles[..., HEAD_SIZE:],
            preferred_element_type=jnp.float32,
        )
        return (combined_output / weight_sum.T[:, :, None]).astype(jnp.bfloat16)

    per_block = lax.map(attend, (q_blocks, query_ids))
    outgoing = per_block.reshape(n_seq, local_rows, per_seq * HEAD_SIZE)
    returned = lax.all_to_all(outgoing, "seq", split_axis=0, concat_axis=2, tiled=True)
    return returned.reshape(local_rows, H * HEAD_SIZE)


def solution(mesh):
    return jax.shard_map(
        shards,
        mesh=mesh,
        in_specs=(
            P(("seq", "qblk"), None),
            P(("seq", "qblk"), None),
            P(("seq", "qblk"), None),
            P(),
            P(),
        ),
        out_specs=P(("seq", "qblk"), None),
        check_vma=False,
    )
```

profile of v0, /device:TPU:0, one launch (start us, length us, event | category | flops | bytes accessed | tf_op | source)
XLA Modules:
  0.0 393.2 jit_solution(18062127807680199011)
XLA Ops:
  4.1 7.4 %all-to-all-start.1 = ((bf16[128,8,1024]{0,2,1:T(8,128)(2,1)}), bf16[128,8,1024]{0,2,1:T(8,128)(2,1)S(1)}, u32[]{:S(2)}, u32[]{:S(2)}) async-start(bf16[128,8,1024]{0,2,1:T(8,128)(2,1)} %bitcast.7), calls=%async_computation.1 | async-start | bytes 4194304 | tf_op jit(solution)/shard_map/all_to_all | solution.py:25
  14.6 45.2 %all-to-all-done.1 = bf16[128,8,1024]{0,2,1:T(8,128)(2,1)S(1)} async-done(((bf16[128,8,1024]{0,2,1:T(8,128)(2,1)}), bf16[128,8,1024]{0,2,1:T(8,128)(2,1)S(1)}, u32[]{:S(2)}, u32[]{:S(2)}) %all-to-all-start.1) | async-done | bytes 2097184 | tf_op jit(solution)/shard_map/all_to_all | solution.py:25
  65.8 48.3 %all-to-all-done = bf16[128,32,256]{2,0,1:T(8,128)(2,1)S(1)} async-done(((bf16[128,32,256]{2,0,1:T(8,128)(2,1)}), bf16[128,32,256]{2,0,1:T(8,128)(2,1)S(1)}, u32[]{:S(2)}, u32[]{:S(2)}) %all-to-all-start) | async-done | bytes 2097184 | tf_op jit(solution)/shard_map/all_to_all | solution.py:38
  114.2 218.2 %while.12 = (s32[]{:T(128)}, bf16[8,128,8,128]{1,3,2,0:T(8,128)(2,1)}, s32[8]{0:T(128)S(1)}, s32[8,32,16]{2,0,1:T(8,128)S(1)}, bf16[32,128,256]{2,1,0:T(8,128)(2...) while((s32[]{:T(128)}, ...), condition=%wide.region_3.4_spmd.clone.clone, body=%wide.region_0.3_spmd.clone.clone.sunk | while | flops 1109671680 | bytes 76317896 | solution.py:77
  123.8 7.4 %fusion.57 = (f32[8,128]{1,0:T(8,128)S(1)}, f32[8,128,16,128]{1,3,2,0:T(8,128)S(1)}) fusion(s32[128]{0:T(128)S(1)} %iota_add_fusion.4, s32[8,16,128]{2,1,0:T(8,128)S(1)} %iota_add_fusion.5, pred[8,16]{1,0:T(8,128)(4,1)S(1)} %iota_compare_fusion.2, bf16[8,16,128,256]{3,2,1,0:T(8,128)(2,1)} %bitcast.77, ...), kind=kOutput, calls=%fused_computation.8.clone.1 | convolution fusion | flops 547355648 | bytes 12915840 | tf_op jit(solution)/shard_map/while/body/eval_jaxpr/qhd,hmkd->hqmk/dot_general | solution.py:54
  134.8 6.5 %fusion.59 = bf16[8,128,8,128]{1,3,2,0:T(8,128)(2,1)} fusion(bf16[8,128,8,128]{1,3,2,0:T(8,128)(2,1)} %get-tuple-element.198, s32[]{:T(128)} %get-tuple-element.197, f32[8,128,16,128]{1,3,2,0:T(8,128)S(1)} %get-tuple-element.184, f32[8,128]{1,0:T(8,128)S(1)} %get-tuple-element.185, s32[128]{0:T(128)S(1)} %iota_add_fusion.4, ...), kind=kOutput, calls=%fused_computation.22.clone.1 | convolution fusion | flops 549715968 | bytes 12920832 | tf_op jit(solution)/shard_map/while/body/eval_jaxpr/hqmk,hmkd->qhd/dot_general | solution.py:69
  151.0 7.4 %fusion.57 = (f32[8,128]{1,0:T(8,128)S(1)}, f32[8,128,16,128]{1,3,2,0:T(8,128)S(1)}) fusion(s32[128]{0:T(128)S(1)} %iota_add_fusion.4, s32[8,16,128]{2,1,0:T(8,128)S(1)} %iota_add_fusion.5, pred[8,16]{1,0:T(8,128)(4,1)S(1)} %iota_compare_fusion.2, bf16[8,16,128,256]{3,2,1,0:T(8,128)(2,1)} %bitcast.77, ...), kind=kOutput, calls=%fused_computation.8.clone.1 | convolution fusion | flops 547355648 | bytes 12915840 | tf_op jit(solution)/shard_map/while/body/eval_jaxpr/qhd,hmkd->hqmk/dot_general | solution.py:54
  162.0 6.5 %fusion.59 = bf16[8,128,8,128]{1,3,2,0:T(8,128)(2,1)} fusion(bf16[8,128,8,128]{1,3,2,0:T(8,128)(2,1)} %get-tuple-element.198, s32[]{:T(128)} %get-tuple-element.197, f32[8,128,16,128]{1,3,2,0:T(8,128)S(1)} %get-tuple-element.184, f32[8,128]{1,0:T(8,128)S(1)} %get-tuple-element.185, s32[128]{0:T(128)S(1)} %iota_add_fusion.4, ...), kind=kOutput, calls=%fused_computation.22.clone.1 | convolution fusion | flops 549715968 | bytes 12920832 | tf_op jit(solution)/shard_map/while/body/eval_jaxpr/hqmk,hmkd->qhd/dot_general | solution.py:69
  178.2 7.4 %fusion.57 = (f32[8,128]{1,0:T(8,128)S(1)}, f32[8,128,16,128]{1,3,2,0:T(8,128)S(1)}) fusion(s32[128]{0:T(128)S(1)} %iota_add_fusion.4, s32[8,16,128]{2,1,0:T(8,128)S(1)} %iota_add_fusion.5, pred[8,16]{1,0:T(8,128)(4,1)S(1)} %iota_compare_fusion.2, bf16[8,16,128,256]{3,2,1,0:T(8,128)(2,1)} %bitcast.77, ...), kind=kOutput, calls=%fused_computation.8.clone.1 | convolution fusion | flops 547355648 | bytes 12915840 | tf_op jit(solution)/shard_map/while/body/eval_jaxpr/qhd,hmkd->hqmk/dot_general | solution.py:54
  189.2 6.5 %fusion.59 = bf16[8,128,8,128]{1,3,2,0:T(8,128)(2,1)} fusion(bf16[8,128,8,128]{1,3,2,0:T(8,128)(2,1)} %get-tuple-element.198, s32[]{:T(128)} %get-tuple-element.197, f32[8,128,16,128]{1,3,2,0:T(8,128)S(1)} %get-tuple-element.184, f32[8,128]{1,0:T(8,128)S(1)} %get-tuple-element.185, s32[128]{0:T(128)S(1)} %iota_add_fusion.4, ...), kind=kOutput, calls=%fused_computation.22.clone.1 | convolution fusion | flops 549715968 | bytes 12920832 | tf_op jit(solution)/shard_map/while/body/eval_jaxpr/hqmk,hmkd->qhd/dot_general | solution.py:69
  205.5 7.4 %fusion.57 = (f32[8,128]{1,0:T(8,128)S(1)}, f32[8,128,16,128]{1,3,2,0:T(8,128)S(1)}) fusion(s32[128]{0:T(128)S(1)} %iota_add_fusion.4, s32[8,16,128]{2,1,0:T(8,128)S(1)} %iota_add_fusion.5, pred[8,16]{1,0:T(8,128)(4,1)S(1)} %iota_compare_fusion.2, bf16[8,16,128,256]{3,2,1,0:T(8,128)(2,1)} %bitcast.77, ...), kind=kOutput, calls=%fused_computation.8.clone.1 | convolution fusion | flops 547355648 | bytes 12915840 | tf_op jit(solution)/shard_map/while/body/eval_jaxpr/qhd,hmkd->hqmk/dot_general | solution.py:54
  216.5 6.5 %fusion.59 = bf16[8,128,8,128]{1,3,2,0:T(8,128)(2,1)} fusion(bf16[8,128,8,128]{1,3,2,0:T(8,128)(2,1)} %get-tuple-element.198, s32[]{:T(128)} %get-tuple-element.197, f32[8,128,16,128]{1,3,2,0:T(8,128)S(1)} %get-tuple-element.184, f32[8,128]{1,0:T(8,128)S(1)} %get-tuple-element.185, s32[128]{0:T(128)S(1)} %iota_add_fusion.4, ...), kind=kOutput, calls=%fused_computation.22.clone.1 | convolution fusion | flops 549715968 | bytes 12920832 | tf_op jit(solution)/shard_map/while/body/eval_jaxpr/hqmk,hmkd->qhd/dot_general | solution.py:69
  225.5 6.5 %gather_fusion = bf16[128,128,256]{2,1,0:T(8,128)(2,1)} fusion(bf16[32,128,256]{2,1,0:T(8,128)(2,1)S(1)} %get-tuple-element.212, s32[1024]{0:T(1024)S(1)} %pad_clamp_fusion.3), kind=kCustom, calls=%fused_computation.clone.clone.1 | custom fusion | bytes 16777728 | tf_op jit(solution)/shard_map/while/body/eval_jaxpr/gather | solution.py:52
  232.8 7.4 %fusion.57 = (f32[8,128]{1,0:T(8,128)S(1)}, f32[8,128,16,128]{1,3,2,0:T(8,128)S(1)}) fusion(s32[128]{0:T(128)S(1)} %iota_add_fusion.4, s32[8,16,128]{2,1,0:T(8,128)S(1)} %iota_add_fusion.5, pred[8,16]{1,0:T(8,128)(4,1)S(1)} %iota_compare_fusion.2, bf16[8,16,128,256]{3,2,1,0:T(8,128)(2,1)} %bitcast.77, ...), kind=kOutput, calls=%fused_computation.8.clone.1 | convolution fusion | flops 547355648 | bytes 12915840 | tf_op jit(solution)/shard_map/while/body/eval_jaxpr/qhd,hmkd->hqmk/dot_general | solution.py:54
  243.8 6.5 %fusion.59 = bf16[8,128,8,128]{1,3,2,0:T(8,128)(2,1)} fusion(bf16[8,128,8,128]{1,3,2,0:T(8,128)(2,1)} %get-tuple-element.198, s32[]{:T(128)} %get-tuple-element.197, f32[8,128,16,128]{1,3,2,0:T(8,128)S(1)} %get-tuple-element.184, f32[8,128]{1,0:T(8,128)S(1)} %get-tuple-element.185, s32[128]{0:T(128)S(1)} %iota_add_fusion.4, ...), kind=kOutput, calls=%fused_computation.22.clone.1 | convolution fusion | flops 549715968 | bytes 12920832 | tf_op jit(solution)/shard_map/while/body/eval_jaxpr/hqmk,hmkd->qhd/dot_general | solution.py:69
  252.8 6.5 %gather_fusion = bf16[128,128,256]{2,1,0:T(8,128)(2,1)} fusion(bf16[32,128,256]{2,1,0:T(8,128)(2,1)S(1)} %get-tuple-element.212, s32[1024]{0:T(1024)S(1)} %pad_clamp_fusion.3), kind=kCustom, calls=%fused_computation.clone.clone.1 | custom fusion | bytes 16777728 | tf_op jit(solution)/shard_map/while/body/eval_jaxpr/gather | solution.py:52
  260.2 7.4 %fusion.57 = (f32[8,128]{1,0:T(8,128)S(1)}, f32[8,128,16,128]{1,3,2,0:T(8,128)S(1)}) fusion(s32[128]{0:T(128)S(1)} %iota_add_fusion.4, s32[8,16,128]{2,1,0:T(8,128)S(1)} %iota_add_fusion.5, pred[8,16]{1,0:T(8,128)(4,1)S(1)} %iota_compare_fusion.2, bf16[8,16,128,256]{3,2,1,0:T(8,128)(2,1)} %bitcast.77, ...), kind=kOutput, calls=%fused_computation.8.clone.1 | convolution fusion | flops 547355648 | bytes 12915840 | tf_op jit(solution)/shard_map/while/body/eval_jaxpr/qhd,hmkd->hqmk/dot_general | solution.py:54
  271.2 6.5 %fusion.59 = bf16[8,128,8,128]{1,3,2,0:T(8,128)(2,1)} fusion(bf16[8,128,8,128]{1,3,2,0:T(8,128)(2,1)} %get-tuple-element.198, s32[]{:T(128)} %get-tuple-element.197, f32[8,128,16,128]{1,3,2,0:T(8,128)S(1)} %get-tuple-element.184, f32[8,128]{1,0:T(8,128)S(1)} %get-tuple-element.185, s32[128]{0:T(128)S(1)} %iota_add_fusion.4, ...), kind=kOutput, calls=%fused_computation.22.clone.1 | convolution fusion | flops 549715968 | bytes 12920832 | tf_op jit(solution)/shard_map/while/body/eval_jaxpr/hqmk,hmkd->qhd/dot_general | solution.py:69
  280.2 6.5 %gather_fusion = bf16[128,128,256]{2,1,0:T(8,128)(2,1)} fusion(bf16[32,128,256]{2,1,0:T(8,128)(2,1)S(1)} %get-tuple-element.212, s32[1024]{0:T(1024)S(1)} %pad_clamp_fusion.3), kind=kCustom, calls=%fused_computation.clone.clone.1 | custom fusion | bytes 16777728 | tf_op jit(solution)/shard_map/while/body/eval_jaxpr/gather | solution.py:52
  287.6 7.4 %fusion.57 = (f32[8,128]{1,0:T(8,128)S(1)}, f32[8,128,16,128]{1,3,2,0:T(8,128)S(1)}) fusion(s32[128]{0:T(128)S(1)} %iota_add_fusion.4, s32[8,16,128]{2,1,0:T(8,128)S(1)} %iota_add_fusion.5, pred[8,16]{1,0:T(8,128)(4,1)S(1)} %iota_compare_fusion.2, bf16[8,16,128,256]{3,2,1,0:T(8,128)(2,1)} %bitcast.77, ...), kind=kOutput, calls=%fused_computation.8.clone.1 | convolution fusion | flops 547355648 | bytes 12915840 | tf_op jit(solution)/shard_map/while/body/eval_jaxpr/qhd,hmkd->hqmk/dot_general | solution.py:54
  298.6 6.5 %fusion.59 = bf16[8,128,8,128]{1,3,2,0:T(8,128)(2,1)} fusion(bf16[8,128,8,128]{1,3,2,0:T(8,128)(2,1)} %get-tuple-element.198, s32[]{:T(128)} %get-tuple-element.197, f32[8,128,16,128]{1,3,2,0:T(8,128)S(1)} %get-tuple-element.184, f32[8,128]{1,0:T(8,128)S(1)} %get-tuple-element.185, s32[128]{0:T(128)S(1)} %iota_add_fusion.4, ...), kind=kOutput, calls=%fused_computation.22.clone.1 | convolution fusion | flops 549715968 | bytes 12920832 | tf_op jit(solution)/shard_map/while/body/eval_jaxpr/hqmk,hmkd->qhd/dot_general | solution.py:69
  307.6 6.5 %gather_fusion = bf16[128,128,256]{2,1,0:T(8,128)(2,1)} fusion(bf16[32,128,256]{2,1,0:T(8,128)(2,1)S(1)} %get-tuple-element.212, s32[1024]{0:T(1024)S(1)} %pad_clamp_fusion.3), kind=kCustom, calls=%fused_computation.clone.clone.1 | custom fusion | bytes 16777728 | tf_op jit(solution)/shard_map/while/body/eval_jaxpr/gather | solution.py:52
  314.9 7.4 %fusion.57 = (f32[8,128]{1,0:T(8,128)S(1)}, f32[8,128,16,128]{1,3,2,0:T(8,128)S(1)}) fusion(s32[128]{0:T(128)S(1)} %iota_add_fusion.4, s32[8,16,128]{2,1,0:T(8,128)S(1)} %iota_add_fusion.5, pred[8,16]{1,0:T(8,128)(4,1)S(1)} %iota_compare_fusion.2, bf16[8,16,128,256]{3,2,1,0:T(8,128)(2,1)} %bitcast.77, ...), kind=kOutput, calls=%fused_computation.8.clone.1 | convolution fusion | flops 547355648 | bytes 12915840 | tf_op jit(solution)/shard_map/while/body/eval_jaxpr/qhd,hmkd->hqmk/dot_general | solution.py:54
  335.2 52.1 %all_to_all.45 = bf16[8,128,1024]{2,1,0:T(8,128)(2,1)} all-to-all(bf16[8,128,1024]{2,1,0:T(8,128)(2,1)S(1)} %copy.55), channel_id=1, replica_groups=mesh['seq'=8,'qblk'=4] {'seq'}, dimensions={0} | all-to-all | bytes 4194304 | tf_op jit(solution)/shard_map/all_to_all | solution.py:79
  (154 shorter events, 89.4 us)
Async XLA Ops:
  0.0 65.5 %copy-start = (s32[64,32,16]{0,2,1:T(8,128)S(1)}, s32[64,32,16]{0,2,1:T(8,128)}, u32[]{:S(2)}) copy-start(s32[64,32,16]{0,2,1:T(8,128)} %param.12) | copy-start | bytes 393220
  0.0 11.6 %copy-start.2 = (bf16[128,1024]{1,0:T(8,128)(2,1)S(1)}, bf16[128,1024]{1,0:T(8,128)(2,1)}, u32[]{:S(2)}) copy-start(bf16[128,1024]{1,0:T(8,128)(2,1)} %param.10) | copy-start | bytes 786436
  0.0 11.9 %copy-start.3 = (bf16[128,1024]{1,0:T(8,128)(2,1)S(1)}, bf16[128,1024]{1,0:T(8,128)(2,1)}, u32[]{:S(2)}) copy-start(bf16[128,1024]{1,0:T(8,128)(2,1)} %param.11) | copy-start | bytes 786436
  4.1 61.6 %copy-start.4 = (s32[64,32]{0,1:T(8,128)S(1)}, s32[64,32]{0,1:T(8,128)}, u32[]{:S(2)}) copy-start(s32[64,32]{0,1:T(8,128)} %param.13) | copy-start | bytes 24580
  4.1 55.7 %all-to-all-start.1 = ((bf16[128,8,1024]{0,2,1:T(8,128)(2,1)}), bf16[128,8,1024]{0,2,1:T(8,128)(2,1)S(1)}, u32[]{:S(2)}, u32[]{:S(2)}) async-start(bf16[128,8,1024]{0,2,1:T(8,128)(2,1)} %bitcast.7), calls=%async_computation.1 | async-start | bytes 4194304 | tf_op jit(solution)/shard_map/all_to_all | solution.py:25
  59.8 2.0 copy-start.1
  61.8 52.4 %all-to-all-start = ((bf16[128,32,256]{2,0,1:T(8,128)(2,1)}), bf16[128,32,256]{2,0,1:T(8,128)(2,1)S(1)}, u32[]{:S(2)}, u32[]{:S(2)}) async-start(bf16[128,32,256]{2,0,1:T(8,128)(2,1)} %bitcast.81), calls=%async_computation | async-start | bytes 4194304 | tf_op jit(solution)/shard_map/all_to_all | solution.py:38
  123.8 11.0 %slice-start = ((s8[8388608]{0:T(1024)(128)(4,1)}), s8[4194304]{0:T(1024)(128)(4,1)S(1)}, s32[]{:S(2)}) async-start(s8[8388608]{0:T(1024)(128)(4,1)} %bitcast.78), calls=%async_computation.3 | async-start | bytes 8388608 | tf_op jit(solution)/shard_map/while
  123.8 11.0 %slice-start.1 = ((s8[8388608]{0:T(1024)(128)(4,1)}), s8[4194304]{0:T(1024)(128)(4,1)S(1)}, s32[]{:S(2)}) async-start(s8[8388608]{0:T(1024)(128)(4,1)} %bitcast.78), calls=%async_computation.4 | async-start | bytes 8388608 | tf_op jit(solution)/shard_map/while
  150.9 11.0 %slice-start = ((s8[8388608]{0:T(1024)(128)(4,1)}), s8[4194304]{0:T(1024)(128)(4,1)S(1)}, s32[]{:S(2)}) async-start(s8[8388608]{0:T(1024)(128)(4,1)} %bitcast.78), calls=%async_computation.3 | async-start | bytes 8388608 | tf_op jit(solution)/shard_map/while
  150.9 11.0 %slice-start.1 = ((s8[8388608]{0:T(1024)(128)(4,1)}), s8[4194304]{0:T(1024)(128)(4,1)S(1)}, s32[]{:S(2)}) async-start(s8[8388608]{0:T(1024)(128)(4,1)} %bitcast.78), calls=%async_computation.4 | async-start | bytes 8388608 | tf_op jit(solution)/shard_map/while
  178.2 11.0 %slice-start = ((s8[8388608]{0:T(1024)(128)(4,1)}), s8[4194304]{0:T(1024)(128)(4,1)S(1)}, s32[]{:S(2)}) async-start(s8[8388608]{0:T(1024)(128)(4,1)} %bitcast.78), calls=%async_computation.3 | async-start | bytes 8388608 | tf_op jit(solution)/shard_map/while
  178.2 11.0 %slice-start.1 = ((s8[8388608]{0:T(1024)(128)(4,1)}), s8[4194304]{0:T(1024)(128)(4,1)S(1)}, s32[]{:S(2)}) async-start(s8[8388608]{0:T(1024)(128)(4,1)} %bitcast.78), calls=%async_computation.4 | async-start | bytes 8388608 | tf_op jit(solution)/shard_map/while
  205.5 11.0 %slice-start = ((s8[8388608]{0:T(1024)(128)(4,1)}), s8[4194304]{0:T(1024)(128)(4,1)S(1)}, s32[]{:S(2)}) async-start(s8[8388608]{0:T(1024)(128)(4,1)} %bitcast.78), calls=%async_computation.3 | async-start | bytes 8388608 | tf_op jit(solution)/shard_map/while
  205.5 11.0 %slice-start.1 = ((s8[8388608]{0:T(1024)(128)(4,1)}), s8[4194304]{0:T(1024)(128)(4,1)S(1)}, s32[]{:S(2)}) async-start(s8[8388608]{0:T(1024)(128)(4,1)} %bitcast.78), calls=%async_computation.4 | async-start | bytes 8388608 | tf_op jit(solution)/shard_map/while
  232.8 11.0 %slice-start = ((s8[8388608]{0:T(1024)(128)(4,1)}), s8[4194304]{0:T(1024)(128)(4,1)S(1)}, s32[]{:S(2)}) async-start(s8[8388608]{0:T(1024)(128)(4,1)} %bitcast.78), calls=%async_computation.3 | async-start | bytes 8388608 | tf_op jit(solution)/shard_map/while
  232.8 11.0 %slice-start.1 = ((s8[8388608]{0:T(1024)(128)(4,1)}), s8[4194304]{0:T(1024)(128)(4,1)S(1)}, s32[]{:S(2)}) async-start(s8[8388608]{0:T(1024)(128)(4,1)} %bitcast.78), calls=%async_computation.4 | async-start | bytes 8388608 | tf_op jit(solution)/shard_map/while
  260.2 11.0 %slice-start = ((s8[8388608]{0:T(1024)(128)(4,1)}), s8[4194304]{0:T(1024)(128)(4,1)S(1)}, s32[]{:S(2)}) async-start(s8[8388608]{0:T(1024)(128)(4,1)} %bitcast.78), calls=%async_computation.3 | async-start | bytes 8388608 | tf_op jit(solution)/shard_map/while
  260.2 11.0 %slice-start.1 = ((s8[8388608]{0:T(1024)(128)(4,1)}), s8[4194304]{0:T(1024)(128)(4,1)S(1)}, s32[]{:S(2)}) async-start(s8[8388608]{0:T(1024)(128)(4,1)} %bitcast.78), calls=%async_computation.4 | async-start | bytes 8388608 | tf_op jit(solution)/shard_map/while
  287.5 11.0 %slice-start = ((s8[8388608]{0:T(1024)(128)(4,1)}), s8[4194304]{0:T(1024)(128)(4,1)S(1)}, s32[]{:S(2)}) async-start(s8[8388608]{0:T(1024)(128)(4,1)} %bitcast.78), calls=%async_computation.3 | async-start | bytes 8388608 | tf_op jit(solution)/shard_map/while
  287.5 11.0 %slice-start.1 = ((s8[8388608]{0:T(1024)(128)(4,1)}), s8[4194304]{0:T(1024)(128)(4,1)S(1)}, s32[]{:S(2)}) async-start(s8[8388608]{0:T(1024)(128)(4,1)} %bitcast.78), calls=%async_computation.4 | async-start | bytes 8388608 | tf_op jit(solution)/shard_map/while
  314.9 11.0 %slice-start = ((s8[8388608]{0:T(1024)(128)(4,1)}), s8[4194304]{0:T(1024)(128)(4,1)S(1)}, s32[]{:S(2)}) async-start(s8[8388608]{0:T(1024)(128)(4,1)} %bitcast.78), calls=%async_computation.3 | async-start | bytes 8388608 | tf_op jit(solution)/shard_map/while
  314.9 11.0 %slice-start.1 = ((s8[8388608]{0:T(1024)(128)(4,1)}), s8[4194304]{0:T(1024)(128)(4,1)S(1)}, s32[]{:S(2)}) async-start(s8[8388608]{0:T(1024)(128)(4,1)} %bitcast.78), calls=%async_computation.4 | async-start | bytes 8388608 | tf_op jit(solution)/shard_map/while
where the time goes:
time: 395 us; the launch traced here: 393 us
  matrix products  111 us (28%)
  waiting for transfers between devices  93.5 us (24%)
  local copies, waits for them, and re-layouts  74 us (19%)
  blocking collectives  52.1 us (13%)
  other arithmetic  31.2 us (8%)
  loops' own time  20.6 us (5%)
  starting transfers between devices  11.1 us (3%)
    dot_general x8, matrix products, attend(): jnp.einsum('qhd,hmkd->hqmk', q_tile, key_value_tiles[..., :HEAD_SIZE], pr...  58.9 us
    all_to_all x1, blocking collectives, shards(): lax.all_to_all(outgoing, 'seq', split_axis=0, concat_axis=2, tiled=True)  52.1 us
    dot_general x8, matrix products, attend(): jnp.einsum('hqmk,hmkd->qhd', weights.astype(jnp.bfloat16), key_value_tile...  51.6 us
    gather x8, local copies, waits for them, and re-layouts, attend(): key_value_tiles = kv_blocks[indices]  51.3 us
    all_to_all x1, waiting for transfers between devices, shards(): lax.all_to_all(spread, ('seq', 'qblk'), split_axis=1, concat_axis=0, tile...  48.3 us
    all_to_all x1, waiting for transfers between devices, shards(): lax.all_to_all(by_slot, 'seq', split_axis=1, concat_axis=0, tiled=True)  45.2 us
    reduce_sum x8, other arithmetic, attend(): weight_sum = jnp.sum(weights, axis=(2, 3))  28.8 us
    another operation x1, loops' own time, shards(): per_block = lax.map(attend, (q_blocks, query_ids))  20.6 us
  transfers between devices with their start and end apart: 2, of which 2 were waited for; matrix products, arithmetic and copies ran while one was open for 1% of the time, Pallas kernels for 0%

commit v1 on v0

v1 whole, which is shorter than its diff:
```python
import functools

import jax
import jax.numpy as jnp
from jax import lax
from jax.experimental import pallas as pl
from jax.experimental.pallas import tpu as pltpu
from jax.sharding import Mesh, PartitionSpec as P

H = 64
KVH = 8
D = 128
BLK = 128
MAXB = 16
GROUP = H // KVH
HALF = KVH // 2
LOG2E = 1.4426950408889634
C = D ** (-0.5) * LOG2E
NEVER = -4 * BLK


def attend_unit(q, k_at, v_at, thr_at, diff, s_ref):
    top = None
    for j in range(MAXB // 2):
        k = jnp.concatenate([k_at(2 * j), k_at(2 * j + 1)], axis=0)
        s = lax.dot_general(q, k, (((1,), (1,)), ((), ())), preferred_element_type=jnp.float32)
        for i in range(2):
            part = s[:, i * BLK : (i + 1) * BLK]
            part = jnp.where(diff <= thr_at(2 * j + i), part, -jnp.inf)
            s_ref[:, (2 * j + i) * BLK : (2 * j + i + 1) * BLK] = part
            top = part if top is None else jnp.maximum(top, part)
    highest = jnp.max(top, axis=1, keepdims=True) * C
    total = None
    acc = None
    for j in range(MAXB // 2):
        v = jnp.concatenate([v_at(2 * j), v_at(2 * j + 1)], axis=0)
        p = jnp.exp2(s_ref[:, 2 * j * BLK : (2 * j + 2) * BLK] * C - highest)
        both = p[:, :BLK] + p[:, BLK:]
        total = both if total is None else total + both
        o = jnp.dot(p.astype(jnp.bfloat16), v, preferred_element_type=jnp.float32)
        acc = o if acc is None else acc + o
    return (acc / jnp.sum(total, axis=1, keepdims=True)).astype(jnp.bfloat16)


def attend_kernel(idx_ref, thr_ref, qa_ref, qb_ref, kv_ref, oa_ref, ob_ref, s_ref):
    h = pl.program_id(0)
    diff = lax.broadcasted_iota(jnp.int32, (BLK, BLK), 1) - lax.broadcasted_iota(
        jnp.int32, (BLK, BLK), 0
    )
    for n, (q_ref, o_ref) in enumerate(((qa_ref, oa_ref), (qb_ref, ob_ref))):
        base = (h * 2 + n) * MAXB
        o_ref[...] = attend_unit(
            q_ref[...],
            lambda m: kv_ref[idx_ref[base + m], 0],
            lambda m: kv_ref[idx_ref[base + m], 1],
            lambda m: thr_ref[base + m],
            diff,
            s_ref.at[n],
        )


def attend(idx, thr, qa, qb, kv):
    col = pl.BlockSpec((BLK, D), lambda h, *_: (0, h))
    whole = pl.BlockSpec(kv.shape, lambda h, *_: (0, 0, 0, 0))
    out = jax.ShapeDtypeStruct(qa.shape, jnp.bfloat16)
    units = 2 * GROUP * MAXB * BLK * BLK
    return pl.pallas_call(
        attend_kernel,
        grid_spec=pltpu.PrefetchScalarGridSpec(
            num_scalar_prefetch=2,
            grid=(GROUP,),
            in_specs=[col, col, whole],
            out_specs=[col, col],
            scratch_shapes=[pltpu.VMEM((2, BLK, MAXB * BLK), jnp.float32)],
        ),
        out_shape=[out, out],
        cost_estimate=pl.CostEstimate(
            flops=4 * units * D, bytes_accessed=kv.size * 2, transcendentals=units
        ),
        name="attend",
    )(idx, thr, qa, qb, kv)


def shards(q, k, v, block_list, block_count):
    c = lax.axis_index("core")
    chip = lax.axis_index("seq") * lax.axis_size("y") + lax.axis_index("y")
    swap = [(0, 1), (1, 0)]

    def halves(x):
        w = x.shape[1] // 2
        return (
            lax.dynamic_slice_in_dim(x, c * w, w, 1),
            lax.dynamic_slice_in_dim(x, (1 - c) * w, w, 1),
        )

    kv = jnp.stack([k.reshape(BLK, KVH, D), v.reshape(BLK, KVH, D)], axis=0)
    kv = kv.transpose(2, 0, 1, 3).reshape(2, HALF, 2, BLK, D)
    kv_mine = lax.dynamic_index_in_dim(kv, c, 0, keepdims=False)
    kv_sent = lax.dynamic_index_in_dim(kv, 1 - c, 0, keepdims=False)
    kv_got = lax.ppermute(kv_sent, "core", swap)
    qa, q_sent = halves(q)
    qb = lax.ppermute(q_sent, "core", swap)
    pair = jnp.stack([kv_mine, kv_got], axis=1)

    lists = lax.dynamic_slice_in_dim(block_list, c * (H // 2), H // 2, 0)
    counts = lax.dynamic_slice_in_dim(block_count, c * (H // 2), H // 2, 0)
    blocks = jnp.stack([2 * chip + c, 2 * chip + 1 - c])
    lists = jnp.stack([lists[:, blocks[0]], lists[:, blocks[1]]], axis=1)
    counts = jnp.stack([counts[:, blocks[0]], counts[:, blocks[1]]], axis=1)
    slots = jnp.arange(MAXB, dtype=jnp.int32)
    thr = jnp.where(
        slots < counts[:, :, None], (blocks[None, :, None] - lists) * BLK, NEVER
    ).reshape(HALF, -1)
    idx = ((lists // 2) * 2 + (lists % 2 + c) % 2).reshape(HALF, -1)

    oa, ob = [], []
    for g in range(HALF):
        gathered = lax.all_gather(pair[g], ("seq", "y"), axis=0, tiled=True)
        w = GROUP * D
        a, b = attend(
            idx[g], thr[g], qa[:, g * w : (g + 1) * w], qb[:, g * w : (g + 1) * w], gathered
        )
        oa.append(a)
        ob.append(b)
    mine = jnp.concatenate(oa, axis=1)
    got = lax.ppermute(jnp.concatenate(ob, axis=1), "core", swap)
    low = jnp.where(c == 0, mine, got)
    high = jnp.where(c == 0, got, mine)
    return jnp.concatenate([low, high], axis=1)


def solution(mesh):
    n_seq, n_qblk = mesh.devices.shape
    fine = Mesh(mesh.devices.reshape(n_seq, n_qblk // 2, 2), ("seq", "y", "core"))
    rows = P(("seq", "y", "core"), None)
    return jax.shard_map(
        shards,
        mesh=fine,
        in_specs=(rows, rows, rows, P(), P()),
        out_specs=rows,
        check_vma=False,
    )
```

time: 395 us -> 286 us (0.72)
  matrix products: 111 us -> 0 us
  waiting for transfers between devices: 93.5 us -> 201 us
  local copies, waits for them, and re-layouts: 74 us -> 12.8 us
  Pallas kernels: 0 us -> 54 us
  blocking collectives: 52.1 us -> 0 us
  other arithmetic: 31.2 us -> 3.75 us
  loops' own time: 20.6 us -> 0 us
  between operations: 0.13 us -> 13.3 us
  starting transfers between devices: 11.1 us -> 1.19 us
    all_gather x0 -> x4, waiting for transfers between devices: none -> 195 us  [shards(): gathered = lax.all_gather(pair[g], ('seq', 'y'), axis=0, tiled=True)]
    dot_general x16 -> x0, matrix products: 111 us -> none  [the longest x8 58.9 us: attend(): jnp.einsum('qhd,hmkd->hqmk', q_tile, key_value_tiles[..., :HEAD_SIZE], pr...]
    all_to_all x2 -> x0, waiting for transfers between devices: 93.5 us -> none  [the longest x1 48.3 us: shards(): lax.all_to_all(spread, ('seq', 'qblk'), split_axis=1, concat_axis=0, tile...]
    pallas_call x0 -> x4, Pallas kernels: none -> 54 us  [attend(): pl.pallas_call(attend_kernel, grid_spec=pltpu.PrefetchScalarGridSpec(num_...]
    all_to_all x1 -> x0, blocking collectives: 52.1 us -> none  [shards(): lax.all_to_all(outgoing, 'seq', split_axis=0, concat_axis=2, tiled=True)]
    gather x9 -> x0, local copies, waits for them, and re-layouts: 51.8 us -> none  [the longest x8 51.3 us: attend(): key_value_tiles = kv_blocks[indices]]
    reduce_sum x8 -> x0, other arithmetic: 28.8 us -> none  [attend(): weight_sum = jnp.sum(weights, axis=(2, 3))]
    another operation x1 -> x0, loops' own time: 20.6 us -> none  [shards(): per_block = lax.map(attend, (q_blocks, query_ids))]
  transfers between devices with their start and end apart: 2 -> 7, of which waited for: 2 -> 6; matrix products, arithmetic and copies ran while one was open for 1% -> 4% of each run, Pallas kernels for 0% -> 14%
where the time goes in v1:
time: 286 us
  waiting for transfers between devices  201 us (70%)
  Pallas kernels  54 us (19%)
  between operations  13.3 us (5%)
  local copies, waits for them, and re-layouts  12.8 us (4%)
  other arithmetic  3.75 us (1%)
    all_gather x4, waiting for transfers between devices, shards(): gathered = lax.all_gather(pair[g], ('seq', 'y'), axis=0, tiled=True)  195 us
    pallas_call x4, Pallas kernels, attend(): pl.pallas_call(attend_kernel, grid_spec=pltpu.PrefetchScalarGridSpec(num_...  54 us
  transfers between devices with their start and end apart: 7, of which 6 were waited for; matrix products, arithmetic and copies ran while one was open for 4% of the time, Pallas kernels for 14%

profile of v1, /device:TPU:0, one launch (start us, length us, event | category | flops | bytes accessed | tf_op | source)
XLA Modules:
  0.0 285.9 jit_solution(17496638394999153577)
XLA Ops:
  6.5 1.0 copy.25
  7.5 1.0 copy.26
  9.3 1.2 collective-permute-done.1
  10.5 0.8 fusion.1
  11.4 0.7 all-gather.15.cloned.1.call-update
  12.1 0.7 all-gather.11.cloned.1.call-update
  14.0 0.8 fusion.12
  14.9 0.8 constant_dynamic-slice_fusion.6
  15.9 0.6 squeeze.48.idx_ref
  18.0 0.6 squeeze.52.thr_ref
  20.0 0.7 squeeze.41.idx_ref
  21.4 1.0 constant_dynamic-slice_fusion.1
  22.4 2.2 fusion.9
  24.6 50.0 %all-gather.13.cloned.1.call-done = bf16[1,32,2,128,128]{4,3,2,0,1:T(8,128)(2,1)} async-done(((bf16[1,2,2,128,128]{4,3,2,0,1:T(8,128)(2,1)}), bf16[1,32,2,128,128]{4,3,2,0,1:T(8,128)(2,1)}) %all-gather.13.cloned.1.call-update) | async-done | bytes 2097168 | tf_op jit(solution)/shard_map/all_gather | solution.py:118
  74.6 13.5 %attend.6 = (bf16[128,1024]{1,0:T(8,128)(2,1)}, bf16[128,1024]{1,0:T(8,128)(2,1)}) custom-call(s32[256]{0:T(256)} %squeeze.48.idx_ref, s32[256]{0:T(256)} %squeeze.49.thr_ref, bf16[128,1024]{1,0:T(8,128)(2,1)} %get-tuple-element.24.qa_ref, bf16[128,1024]{1,0:T(8,128)(2,1)} %get-tuple-element.29.qb_ref, bf16[32,2,128,128]{3,2,1,0:T(8,128)(2,1)} %bitcast.29), custom_call_target="tpu_custom_call" | custom-call | flops 2147483648 | bytes 2097152 | tf_op jit(solution)/shard_map/attend/pallas_call | solution.py:67
  88.1 48.4 %all-gather.15.cloned.1.call-done = bf16[1,32,2,128,128]{4,3,2,0,1:T(8,128)(2,1)} async-done(((bf16[1,2,2,128,128]{4,3,2,0,1:T(8,128)(2,1)}), bf16[1,32,2,128,128]{4,3,2,0,1:T(8,128)(2,1)}) %all-gather.15.cloned.1.call-update) | async-done | bytes 2097168 | tf_op jit(solution)/shard_map/all_gather | solution.py:118
  136.5 13.5 %attend.7 = (bf16[128,1024]{1,0:T(8,128)(2,1)}, bf16[128,1024]{1,0:T(8,128)(2,1)}) custom-call(s32[256]{0:T(256)} %squeeze.51.idx_ref, s32[256]{0:T(256)} %squeeze.52.thr_ref, bf16[128,1024]{1,0:T(8,128)(2,1)} %get-tuple-element.26.qa_ref, bf16[128,1024]{1,0:T(8,128)(2,1)} %get-tuple-element.28.qb_ref, bf16[32,2,128,128]{3,2,1,0:T(8,128)(2,1)} %bitcast.28), custom_call_target="tpu_custom_call" | custom-call | flops 2147483648 | bytes 2097152 | tf_op jit(solution)/shard_map/attend/pallas_call | solution.py:67
  150.0 48.4 %all-gather.11.cloned.1.call-done = bf16[1,32,2,128,128]{4,3,2,0,1:T(8,128)(2,1)} async-done(((bf16[1,2,2,128,128]{4,3,2,0,1:T(8,128)(2,1)}), bf16[1,32,2,128,128]{4,3,2,0,1:T(8,128)(2,1)}) %all-gather.11.cloned.1.call-update) | async-done | bytes 2097168 | tf_op jit(solution)/shard_map/all_gather | solution.py:118
  198.4 13.5 %attend.5 = (bf16[128,1024]{1,0:T(8,128)(2,1)}, bf16[128,1024]{1,0:T(8,128)(2,1)}) custom-call(s32[256]{0:T(256)} %squeeze.45.idx_ref, s32[256]{0:T(256)} %squeeze.46.thr_ref, bf16[128,1024]{1,0:T(8,128)(2,1)} %get-tuple-element.25.qa_ref, bf16[128,1024]{1,0:T(8,128)(2,1)} %get-tuple-element.30.qb_ref, bf16[32,2,128,128]{3,2,1,0:T(8,128)(2,1)} %bitcast.27), custom_call_target="tpu_custom_call" | custom-call | flops 2147483648 | bytes 2097152 | tf_op jit(solution)/shard_map/attend/pallas_call | solution.py:67
  211.9 48.4 %all-gather.9.cloned.1.call-done = bf16[1,32,2,128,128]{4,3,2,0,1:T(8,128)(2,1)} async-done(((bf16[1,2,2,128,128]{4,3,2,0,1:T(8,128)(2,1)}), bf16[1,32,2,128,128]{4,3,2,0,1:T(8,128)(2,1)}) %all-gather.9.cloned.1.call-update) | async-done | bytes 2097168 | tf_op jit(solution)/shard_map/all_gather | solution.py:118
  260.3 13.6 %attend.4 = (bf16[128,1024]{1,0:T(8,128)(2,1)}, bf16[128,1024]{1,0:T(8,128)(2,1)}) custom-call(s32[256]{0:T(256)} %squeeze.41.idx_ref, s32[256]{0:T(256)} %squeeze.42.thr_ref, bf16[128,1024]{1,0:T(8,128)(2,1)} %get-tuple-element.23.qa_ref, bf16[128,1024]{1,0:T(8,128)(2,1)} %get-tuple-element.27.qb_ref, bf16[32,2,128,128]{3,2,1,0:T(8,128)(2,1)} %bitcast.26), custom_call_target="tpu_custom_call" | custom-call | flops 2147483648 | bytes 2097152 | tf_op jit(solution)/shard_map/attend/pallas_call | solution.py:67
  273.9 1.1 pad_maximum_fusion.1
  275.3 2.5 collective-permute-done.2
  277.9 1.5 pad_maximum_fusion
  (52 shorter events, 6.2 us)
Async XLA Ops:
  6.5 68.0 %all-gather.13.cloned.1.call-start = ((), (), s32[]{:S(2)}) async-start(), calls=%async_computation.2 | async-start | bytes 2228224 | tf_op jit(solution)/shard_map/all_gather | solution.py:118
  8.6 4.8 %copy-start = (bf16[128,8192]{1,0:T(8,128)(2,1)S(1)}, bf16[128,8192]{1,0:T(8,128)(2,1)}, u32[]{:S(2)}) copy-start(bf16[128,8192]{1,0:T(8,128)(2,1)} %param.5) | copy-start | bytes 6291460
  8.8 1.7 collective-permute-start.1
  11.3 125.1 %all-gather.15.cloned.1.call-start = ((), (), s32[]{:S(2)}) async-start(), calls=%async_computation.3 | async-start | bytes 2228224 | tf_op jit(solution)/shard_map/all_gather | solution.py:118
  12.1 186.3 %all-gather.11.cloned.1.call-start = ((), (), s32[]{:S(2)}) async-start(), calls=%async_computation.1 | async-start | bytes 2228224 | tf_op jit(solution)/shard_map/all_gather | solution.py:118
  12.8 247.5 %all-gather.9.cloned.1.call-start = ((), (), s32[]{:S(2)}) async-start(), calls=%async_computation | async-start | bytes 2228224 | tf_op jit(solution)/shard_map/all_gather | solution.py:118
  13.5 8.9 %collective-permute-start = (bf16[128,4096]{1,0:T(8,128)(2,1)S(1)}, bf16[128,4096]{1,0:T(8,128)(2,1)}, u32[]{:S(2)}, u32[]{:S(2)}) collective-permute-start(bf16[128,4096]{1,0:T(8,128)(2,1)S(1)} %constant_dynamic-slice_fusion.3), channel_id=1, source_target_pairs={{0,1},{1,0},{2,3},{3,2},{4,5},{5,4},{6,7},{7,6},{8,9},{9,8},{10,11... | collective-permute-start | bytes 3145736 | tf_op jit(solution)/shard_map/ppermute | solution.py:102
  260.3 13.6 %copy-start.5 = (bf16[128,1024]{1,0:T(8,128)(2,1)S(1)}, bf16[128,1024]{1,0:T(8,128)(2,1)}, u32[]{:S(2)}) copy-start(bf16[128,1024]{1,0:T(8,128)(2,1)} %get-tuple-element.19) | copy-start | bytes 786436
  260.3 13.7 %copy-start.6 = (bf16[128,1024]{1,0:T(8,128)(2,1)S(1)}, bf16[128,1024]{1,0:T(8,128)(2,1)}, u32[]{:S(2)}) copy-start(bf16[128,1024]{1,0:T(8,128)(2,1)} %get-tuple-element.20) | copy-start | bytes 786436
  260.3 13.7 %copy-start.7 = (bf16[128,1024]{1,0:T(8,128)(2,1)S(1)}, bf16[128,1024]{1,0:T(8,128)(2,1)}, u32[]{:S(2)}) copy-start(bf16[128,1024]{1,0:T(8,128)(2,1)} %get-tuple-element.18) | copy-start | bytes 786436
  273.9 1.2 copy-start.4
  273.9 1.3 copy-start.3
  273.9 1.3 copy-start.1
  273.9 1.3 copy-start.2
  275.1 2.7 collective-permute-start.2
Sparse Core Ops, SparseCore 0:
  11.5 63.0 all-gather.12
  77.3 59.1 all-gather.14
  139.2 59.1 all-gather.10
  201.0 59.2 all-gather.8

commit v2 on v1

--- a/solution.py
+++ b/solution.py
@@ -42,43 +42,178 @@
     return (acc / jnp.sum(total, axis=1, keepdims=True)).astype(jnp.bfloat16)
 
 
-def attend_kernel(idx_ref, thr_ref, qa_ref, qb_ref, kv_ref, oa_ref, ob_ref, s_ref):
-    h = pl.program_id(0)
+ORDERS = ((0, 1, 2), (0, 2, 1), (0, 1, 2), (0, 2, 1), (1, 2, 0), (2, 1, 0), (0, 1, 2), (0, 2, 1))
+SKEW = 2
+
+
+def fused_kernel(sizes, idx_ref, thr_ref, qa_ref, qb_ref, pair_ref, oa_ref, ob_ref, *scratch):
+    bufs = scratch[: 2 * HALF]
+    s_ref, own_sem, send_sem, recv_sem = scratch[2 * HALF :]
+    nb, ny = sizes[1], sizes[2]
+    seq = lax.axis_index("seq")
+    me = (seq // nb, seq % nb, lax.axis_index("y"))
+
+    def target(dim, to):
+        if dim == 2:
+            return {"y": to}
+        return {"seq": to * nb + me[1] if dim == 0 else me[0] * nb + to}
+
+    barrier = pltpu.get_barrier_semaphore()
+    expected = 0
+    for dim in range(3):
+        for way in (1, -1):
+            to = me[dim] + way
+            there = (to >= 0) & (to < sizes[dim])
+            expected = expected + there.astype(jnp.int32)
+
+            @pl.when(there)
+            def _():
+                pl.semaphore_signal(
+                    barrier, inc=1, device_id=target(dim, to), device_id_type=pl.DeviceIdType.MESH
+                )
+
+    own = []
+    for u in range(2 * HALF):
+        copy = pltpu.make_async_copy(
+            pair_ref.at[u // 2, u % 2], bufs[u].at[me[0], me[1], me[2]], own_sem.at[u]
+        )
+        copy.start()
+        own.append(copy)
+    pl.semaphore_wait(barrier, expected)
+
+    offsets = {}
+    slots = 0
+    for u in range(2 * HALF):
+        for dim in range(3):
+            offsets[u, dim] = slots
+            slots += 2 * (sizes[dim] - 1)
+
+    def copy_of(u, stage, way, k):
+        dim = ORDERS[u][stage]
+        done = ORDERS[u][:stage]
+        piece = me[dim] - way * k
+        region = tuple(
+            slice(None) if d in done else (piece if d == dim else me[d]) for d in range(3)
+        )
+        slot = offsets[u, dim] + 2 * k + (0 if way == 1 else 1)
+        sent = (me[dim] + way >= 0) & (me[dim] + way < sizes[dim])
+        held = (piece >= 0) & (piece < sizes[dim])
+        came = me[dim] - way * (k + 1)
+        return (
+            pltpu.make_async_remote_copy(
+                src_ref=bufs[u].at[region],
+                dst_ref=bufs[u].at[region],
+                send_sem=send_sem.at[slot],
+                recv_sem=recv_sem.at[slot],
+                device_id=target(dim, me[dim] + way),
+                device_id_type=pl.DeviceIdType.MESH,
+            ),
+            sent & held,
+            (came >= 0) & (came < sizes[dim]),
+        )
+
+    def send(u, stage, k):
+        for way in (1, -1):
+            copy, sends, _ = copy_of(u, stage, way, k)
+            pl.when(sends)(copy.start)
+
+    def receive(u, stage, k):
+        for way in (1, -1):
+            copy, _, comes = copy_of(u, stage, way, k)
+            pl.when(comes)(copy.wait_recv)
+
+    plans = []
+    for u in range(2 * HALF):
+        plan = [(None, None, 0, 0)]
+        for stage in range(3):
+            n = sizes[ORDERS[u][stage]]
+            for k in range(n - 1):
+                after = (stage, k + 1) if k + 1 < n - 1 else (stage + 1, 0)
+                plan.append((stage, k, *after))
+        plans.append(plan)
+
+    def advance(u, i):
+        stage, k, next_stage, next_k = plans[u][i]
+        if stage is None:
+            own[u].wait()
+        else:
+            receive(u, stage, k)
+        if next_stage < 3:
+            send(u, next_stage, next_k)
+
     diff = lax.broadcasted_iota(jnp.int32, (BLK, BLK), 1) - lax.broadcasted_iota(
         jnp.int32, (BLK, BLK), 0
     )
-    for n, (q_ref, o_ref) in enumerate(((qa_ref, oa_ref), (qb_ref, ob_ref))):
-        base = (h * 2 + n) * MAXB
-        o_ref[...] = attend_unit(
-            q_ref[...],
-            lambda m: kv_ref[idx_ref[base + m], 0],
-            lambda m: kv_ref[idx_ref[base + m], 1],
-            lambda m: thr_ref[base + m],
-            diff,
-            s_ref.at[n],
-        )
-
-
-def attend(idx, thr, qa, qb, kv):
-    col = pl.BlockSpec((BLK, D), lambda h, *_: (0, h))
-    whole = pl.BlockSpec(kv.shape, lambda h, *_: (0, 0, 0, 0))
+
+    def attend(g, low, high):
+        def at(buf, i):
+            return buf[i // (2 * nb * ny), (i // (2 * ny)) % nb, (i // 2) % ny, i % 2]
+
+        def step(h, _):
+            cols = pl.ds(pl.multiple_of(h * D, D), D)
+            for n, (q_ref, o_ref) in enumerate(((qa_ref, oa_ref), (qb_ref, ob_ref))):
+                base = (h * 2 + n) * MAXB
+                at_slot = [idx_ref[base + m].astype(jnp.uint32) for m in range(MAXB)]
+                o_ref[:, cols] = attend_unit(
+                    q_ref[:, cols],
+                    lambda m: at(bufs[2 * g], at_slot[m]),
+                    lambda m: at(bufs[2 * g + 1], at_slot[m]),
+                    lambda m: thr_ref[base + m],
+                    diff,
+                    s_ref.at[n],
+                )
+            return 0
+
+        lax.fori_loop(g * GROUP + low, g * GROUP + high, step, 0)
+
+    length = len(plans[0])
+    last = (HALF - 1) * SKEW + length
+    todo = []
+    for wave in range(last):
+        if todo:
+            attend(*todo.pop(0))
+        for g in range(HALF):
+            i = wave - g * SKEW
+            if 0 <= i < length:
+                advance(2 * g, i)
+                advance(2 * g + 1, i)
+                if i == length - 1:
+                    step = GROUP // SKEW
+                    todo += [(g, j * step, (j + 1) * step) for j in range(SKEW)]
+    g = HALF - 1
+    for item in todo[:-SKEW]:
+        attend(*item)
+    attend(g, 0, GROUP)
+
+    for u in range(2 * HALF):
+        for stage in range(3):
+            for k in range(sizes[ORDERS[u][stage]] - 1):
+                for way in (1, -1):
+                    copy, sends, _ = copy_of(u, stage, way, k)
+                    pl.when(sends)(copy.wait_send)
+
+
+def fused(sizes, idx, thr, qa, qb, pair):
+    vmem = pl.BlockSpec(memory_space=pltpu.VMEM)
+    smem = pl.BlockSpec(memory_space=pltpu.SMEM)
     out = jax.ShapeDtypeStruct(qa.shape, jnp.bfloat16)
-    units = 2 * GROUP * MAXB * BLK * BLK
+    buf = pltpu.VMEM((*sizes, 2, BLK, D), jnp.bfloat16)
+    slots = 2 * HALF * 2 * (sum(sizes) - 3)
     return pl.pallas_call(
-        attend_kernel,
-        grid_spec=pltpu.PrefetchScalarGridSpec(
-            num_scalar_prefetch=2,
-            grid=(GROUP,),
-            in_specs=[col, col, whole],
-            out_specs=[col, col],
-            scratch_shapes=[pltpu.VMEM((2, BLK, MAXB * BLK), jnp.float32)],
-        ),
+        functools.partial(fused_kernel, sizes),
+        in_specs=[smem, smem, vmem, vmem, vmem],
+        out_specs=[vmem, vmem],
+        scratch_shapes=[buf] * (2 * HALF)
+        + [
+            pltpu.VMEM((2, BLK, MAXB * BLK), jnp.float32),
+            pltpu.SemaphoreType.DMA((2 * HALF,)),
+            pltpu.SemaphoreType.DMA((slots,)),
+            pltpu.SemaphoreType.DMA((slots,)),
+        ],
         out_shape=[out, out],
-        cost_estimate=pl.CostEstimate(
-            flops=4 * units * D, bytes_accessed=kv.size * 2, transcendentals=units
-        ),
-        name="attend",
-    )(idx, thr, qa, qb, kv)
+        compiler_params=pltpu.CompilerParams(collective_id=0, has_side_effects=True),
+        name="gather_attend",
+    )(idx, thr, qa, qb, pair)
 
 
 def shards(q, k, v, block_list, block_count):
@@ -100,7 +235,7 @@
     kv_got = lax.ppermute(kv_sent, "core", swap)
     qa, q_sent = halves(q)
     qb = lax.ppermute(q_sent, "core", swap)
-    pair = jnp.stack([kv_mine, kv_got], axis=1)
+    pair = jnp.stack([kv_mine, kv_got], axis=2)
 
     lists = lax.dynamic_slice_in_dim(block_list, c * (H // 2), H // 2, 0)
     counts = lax.dynamic_slice_in_dim(block_count, c * (H // 2), H // 2, 0)
@@ -110,20 +245,12 @@
     slots = jnp.arange(MAXB, dtype=jnp.int32)
     thr = jnp.where(
         slots < counts[:, :, None], (blocks[None, :, None] - lists) * BLK, NEVER
-    ).reshape(HALF, -1)
-    idx = ((lists // 2) * 2 + (lists % 2 + c) % 2).reshape(HALF, -1)
-
-    oa, ob = [], []
-    for g in range(HALF):
-        gathered = lax.all_gather(pair[g], ("seq", "y"), axis=0, tiled=True)
-        w = GROUP * D
-        a, b = attend(
-            idx[g], thr[g], qa[:, g * w : (g + 1) * w], qb[:, g * w : (g + 1) * w], gathered
-        )
-        oa.append(a)
-        ob.append(b)
-    mine = jnp.concatenate(oa, axis=1)
-    got = lax.ppermute(jnp.concatenate(ob, axis=1), "core", swap)
+    ).reshape(-1)
+    idx = ((lists // 2) * 2 + (lists % 2 + c) % 2).reshape(-1)
+
+    nb = lax.axis_size("seq") // 4
+    mine, sent = fused((4, nb, lax.axis_size("y")), idx, thr, qa, qb, pair)
+    got = lax.ppermute(sent, "core", swap)
     low = jnp.where(c == 0, mine, got)
     high = jnp.where(c == 0, got, mine)
     return jnp.concatenate([low, high], axis=1)

time: 286 us -> 129 us (0.45)
  waiting for transfers between devices: 201 us -> 2.86 us
  Pallas kernels: 54 us -> 113 us
  between operations: 13.3 us -> 0.08 us
  local copies, waits for them, and re-layouts: 12.8 us -> 7.27 us
    all_gather x4 -> x0, waiting for transfers between devices: 195 us -> none  [shards(): gathered = lax.all_gather(pair[g], ('seq', 'y'), axis=0, tiled=True)]
    pallas_call x4 -> x1, Pallas kernels: 54 us -> 113 us  [fused(): pl.pallas_call(functools.partial(fused_kernel, sizes), in_specs=[smem, sm...]
    squeeze x8 -> x0, local copies, waits for them, and re-layouts: 4.97 us -> none  [the longest x4 2.51 us: shards(): idx[g]]
    slice x11 -> x0, local copies, waits for them, and re-layouts: 3.88 us -> none  [the longest x1 2.23 us: shards(): qb[:, g * w:(g + 1) * w]]
  transfers between devices with their start and end apart: 7 -> 3, of which waited for: 6 -> 1; matrix products, arithmetic and copies ran while one was open for 4% -> 5% of each run, Pallas kernels for 14% -> 0%
where the time goes in v2:
time: 129 us
  Pallas kernels  113 us (88%)
  local copies, waits for them, and re-layouts  7.27 us (6%)
  other arithmetic  5.53 us (4%)
  waiting for transfers between devices  2.86 us (2%)
    pallas_call x1, Pallas kernels, fused(): pl.pallas_call(functools.partial(fused_kernel, sizes), in_specs=[smem, sm...  113 us
    unnamed x6, local copies, waits for them, and re-layouts  3.11 us
    ppermute x1, waiting for transfers between devices, shards(): got = lax.ppermute(sent, 'core', swap)  2.85 us
  transfers between devices with their start and end apart: 3, of which 1 were waited for; matrix products, arithmetic and copies ran while one was open for 5% of the time, Pallas kernels for 0%

profile of v2, /device:TPU:0, one launch (start us, length us, event | category | flops | bytes accessed | tf_op | source)
XLA Modules:
  0.0 128.9 jit_solution(18438439890764699952)
XLA Ops:
  0.0 1.1 copy.11
  1.1 1.0 copy.12
  2.2 0.1 copy.10
  2.3 0.7 dynamic-slice_bitcast_fusion.1
  3.1 0.5 collective-permute-start.1
  3.6 1.2 constant_dynamic-slice_fusion
  4.7 0.8 fusion.6
  5.6 0.1 copy.9
  5.7 0.8 constant_dynamic-slice_fusion.3
  6.5 0.1 iota_compare_fusion
  6.6 0.1 pad_add_fusion.2
  6.6 0.1 lt.60
  6.7 0.1 copy.8
  6.8 0.1 stack.30
  6.9 0.1 sub.26
  7.0 0.1 sub.27
  7.1 0.6 multiply_select_fusion
  7.7 1.8 %pad_maximum_fusion.1.pair_ref = bf16[4,2,2,128,128]{4,3,2,1,0:T(8,128)(2,1)} fusion(bf16[4,2,1,128,128]{4,3,2,1,0:T(8,128)(2,1)} %bitcast.6, bf16[4,2,1,128,128]{4,3,2,1,0:T(8,128)(2,1)S(1)} %get-tuple-element.13), kind=kLoop, calls=%fused_computation.4 | loop fusion | flops 262144 | bytes 1048576 | tf_op jit(solution)/shard_map/stack | solution.py:238
  9.6 1.0 copy-done.1
  10.5 112.6 %gather_attend.1 = (bf16[128,4096]{1,0:T(8,128)(2,1)}, bf16[128,4096]{1,0:T(8,128)(2,1)}) custom-call(s32[1024]{0:T(1024)} %get-tuple-element.20.idx_ref, s32[1024]{0:T(1024)} %get-tuple-element.19.thr_ref, bf16[128,4096]{1,0:T(8,128)(2,1)} %get-tuple-element.12.qa_ref, bf16[128,4096]{1,0:T(8,128)(2,1)} %copy-done.1, ...), custom_call_target="tpu_custom_call" | custom-call | tf_op jit(solution)/shard_map/gather_attend/pallas_call | solution.py:202
  123.1 0.1 collective-permute-start.2
  123.2 2.9 %collective-permute-done.2 = bf16[128,4096]{1,0:T(8,128)(2,1)S(1)} collective-permute-done((bf16[128,4096]{1,0:T(8,128)(2,1)}, bf16[128,4096]{1,0:T(8,128)(2,1)S(1)}, u32[]{:S(2)}, u32[]{:S(2)}) %collective-permute-start.2) | collective-permute-done | bytes 1048608 | tf_op jit(solution)/shard_map/ppermute | solution.py:253
  126.1 1.4 %broadcast_select_fusion.1 = (bf16[128,4096]{1,0:T(8,128)(2,1)S(1)}, bf16[128,4096]{1,0:T(8,128)(2,1)S(1)}) fusion(bf16[128,4096]{1,0:T(8,128)(2,1)} %get-tuple-element.7, bf16[128,4096]{1,0:T(8,128)(2,1)S(1)} %collective-permute-done.2, pred[]{:T(512)S(6)} %eq.7), kind=kLoop, calls=%fused_computation.2 | loop fusion | flops 1048576 | bytes 4194305 | tf_op jit(solution)/shard_map/jit(_where)/select_n | solution.py:254
  127.4 1.5 %pad_maximum_fusion = bf16[128,8192]{1,0:T(8,128)(2,1)} fusion(bf16[128,4096]{1,0:T(8,128)(2,1)S(1)} %get-tuple-element.10, bf16[128,4096]{1,0:T(8,128)(2,1)S(1)} %get-tuple-element.9), kind=kLoop, calls=%fused_computation | loop fusion | flops 4194304 | bytes 4194304 | tf_op jit(solution)/shard_map/concatenate | solution.py:256
  (9 shorter events, 0.1 us)
Async XLA Ops:
  0.0 3.6 %copy-start = (bf16[128,8192]{1,0:T(8,128)(2,1)S(1)}, bf16[128,8192]{1,0:T(8,128)(2,1)}, u32[]{:S(2)}) copy-start(bf16[128,8192]{1,0:T(8,128)(2,1)} %param.5) | copy-start | bytes 6291460
  3.1 4.7 %collective-permute-start.1 = (bf16[4,2,128,128]{3,2,1,0:T(8,128)(2,1)}, bf16[4,2,128,128]{3,2,1,0:T(8,128)(2,1)}, u32[]{:S(2)}, u32[]{:S(2)}) collective-permute-start(bf16[4,2,128,128]{3,2,1,0:T(8,128)(2,1)} %get-tuple-element.14), channel_id=1, source_target_pairs={{0,1},{1,0},{2,3},{3,2},{4,5},{5,4},{6,7},{7,6},{8,9},{9,8},{10,11... | collective-permute-start | bytes 786440 | tf_op jit(solution)/shard_map/ppermute | solution.py:235
  4.7 4.8 %collective-permute-start = (bf16[128,4096]{1,0:T(8,128)(2,1)S(1)}, bf16[128,4096]{1,0:T(8,128)(2,1)S(1)}, u32[]{:S(2)}, u32[]{:S(2)}) collective-permute-start(bf16[128,4096]{1,0:T(8,128)(2,1)S(1)} %get-tuple-element.11), channel_id=1, source_target_pairs={{0,1},{1,0},{2,3},{3,2},{4,5},{5,4},{6,7},{7,6},{8,9},{9,8},{10,11... | collective-permute-start | bytes 3145736 | tf_op jit(solution)/shard_map/ppermute | solution.py:237
  9.6 1.0 copy-start.1
  123.1 2.9 %collective-permute-start.2 = (bf16[128,4096]{1,0:T(8,128)(2,1)}, bf16[128,4096]{1,0:T(8,128)(2,1)S(1)}, u32[]{:S(2)}, u32[]{:S(2)}) collective-permute-start(bf16[128,4096]{1,0:T(8,128)(2,1)} %get-tuple-element.8), channel_id=1, source_target_pairs={{0,1},{1,0},{2,3},{3,2},{4,5},{5,4},{6,7},{7,6},{8,9},{9,8},{10,11... | collective-permute-start | bytes 3145736 | tf_op jit(solution)/shard_map/ppermute | solution.py:253
